TPU v7x, 32 devices: a whole 2x2x4 slice. The times are simulated.
32 devices in a mesh: groups: 2 (over y), tile: 4 (over z), sect: 2 (over x), half: 2 (over core).
Axes of the slice: x: 2, y: 2, z: 4, core: 2. Of those that a mesh axis runs over, the one named last changes fastest.
Arguments:
- patches: bfloat16 [4, 4, 32, 256, 256], P(('groups', 'sect'), 'tile', 'half'), parts along dimension 0, may hold values from -6 to 6
- pair_lists: int32 [3, 4, 4, 24], P(None, ('groups', 'sect'), 'tile', 'half'), parts along dimension 1, may hold values from 0 to 15, as said below
- move_plan: int32 [2, 4, 4, 24], P(None, ('groups', 'sect'), 'tile', 'half'), parts along dimension 1, may hold values from -1 to 5, as said below
Outputs:
- work_surfaces: float32 [4, 4, 12, 256, 256], P(('groups', 'sect'), 'tile', 'half'), parts along dimension 0
- peak_values: float32 [4, 4, 24], P(('groups', 'sect'), 'tile', 'half'), parts along dimension 0
There are 2 independent parts, one for each index of `groups`. A program takes and returns all parts, laid end to end along the dimension named above; each array names one. Nothing has to cross between parts.
Inputs may be any that keep to these rules, and one draw needn't show every extreme that they name: `pair_lists`: kind 0 names the tile row below (r + 1), kind 1 the next section (s + 1). Every slot of the last tile row has kind 1 and every slot of the last section kind 0; the device of the last tile row in the last section has no live slot. Entries a and b are below 16. `move_plan`: entry 0 is the target tile row of a slot (-1 for unused), entry 1 its work slot there (-1 for unused). A device has at most 12 live slots and at most 3 live slots with the same target; within one section and column half no two live slots share a target and a work slot, work slots are below 6, and live slots are all assigned. Some device has 12 live slots and some target receives 6.
All inputs are finite; a program needn't handle non-finite values.
Results may differ from a plain program's by a relative error of at most 0.0003.
Values may be sent and summed in bfloat16 or wider, within the bound.
A program may use at most 64 MiB of HBM per device.

v0:
```python
import math

import jax
import jax.numpy as jnp
from jax import lax
from jax.sharding import PartitionSpec as P

FLOOR = 0.05


def passed_along(value, axis, steps):
    count = lax.axis_size(axis)
    leading, last = (max(0, -steps), min(count, count - steps))
    return lax.ppermute(value, axis, [(source, source + steps) for source in range(leading, last)])


def split_table(table):
    upper_part = table.astype(jnp.bfloat16)
    widened = lax.optimization_barrier(upper_part).astype(jnp.float32)
    lower_part = (table - widened).astype(jnp.bfloat16)
    return (upper_part, lower_part)


def transform_tables(length):
    indices = jnp.arange(length, dtype=jnp.int32)
    phase_index = indices[:, None] * indices[None, :] % length
    angles = phase_index.astype(jnp.float32) * (2.0 * math.pi / length)
    cosine_table = jnp.cos(angles)
    sine_table = jnp.sin(angles)
    return (cosine_table, sine_table, split_table(cosine_table), split_table(sine_table))


def matmul(left, right):
    return jnp.dot(left, right, precision=lax.Precision.HIGH, preferred_element_type=jnp.float32)


def narrow_product(picture, pieces):
    return jnp.dot(picture, pieces[0], preferred_element_type=jnp.float32) + jnp.dot(
        picture, pieces[1], preferred_element_type=jnp.float32
    )


def spectrum(picture, tables):
    cosine_table, sine_table, cosine_pieces, sine_pieces = tables
    right_cos = narrow_product(picture, cosine_pieces)
    right_sin = narrow_product(picture, sine_pieces)
    real_part = matmul(cosine_table, right_cos) - matmul(sine_table, right_sin)
    imag_part = -(matmul(sine_table, right_cos) + matmul(cosine_table, right_sin))
    return (real_part, imag_part)


def correlate(couple, tables):
    cosine_table, sine_table = (tables[0], tables[1])
    length = couple.shape[-1]
    first_re, first_im = spectrum(couple[0], tables)
    second_re, second_im = spectrum(couple[1], tables)
    cross_re = first_re * second_re + first_im * second_im
    cross_im = first_im * second_re - first_re * second_im
    divisor = jnp.maximum(
        jnp.sqrt(cross_re * cross_re + cross_im * cross_im), FLOOR * length * length
    )
    norm_re = cross_re / divisor
    norm_im = cross_im / divisor
    upper = matmul(norm_re, cosine_table) - matmul(norm_im, sine_table)
    lower = matmul(norm_re, sine_table) + matmul(norm_im, cosine_table)
    return (matmul(cosine_table, upper) - matmul(sine_table, lower)) / length


def settle(arrived_place, lane_ids, work_ids):
    matches = arrived_place[None, :] == work_ids[:, None]
    present = jnp.any(matches, axis=1)
    picked = jnp.sum(jnp.where(matches, lane_ids[None, :], 0), axis=1)
    return (present, picked)


def body(patches, pair_lists, move_plan):
    own_patches = patches[0, 0]
    from_below = passed_along(own_patches, "tile", -1)
    from_next = passed_along(own_patches, "sect", -1)
    pair_kinds = pair_lists[0, 0, 0]
    first_index = pair_lists[1, 0, 0]
    second_index = pair_lists[2, 0, 0]
    targets = move_plan[0, 0, 0]
    places = move_plan[1, 0, 0]
    slot_count = pair_kinds.shape[0]
    patch_count = own_patches.shape[0]
    work_count = slot_count // 2
    tile_count = lax.axis_size("tile")
    per_peer = (slot_count + tile_count - 1) // tile_count
    lane_total = tile_count * per_peer
    tables = transform_tables(own_patches.shape[-1])
    slot_alive = targets >= 0
    firsts = jnp.take(own_patches, first_index, axis=0)
    partners = jnp.concatenate([from_below, from_next], axis=0)
    seconds = jnp.take(partners, pair_kinds * patch_count + second_index, axis=0)
    pair_stack = jnp.stack([firsts, seconds], axis=1)
    slot_order = jnp.arange(slot_count, dtype=jnp.int32)
    earlier = (
        (targets[:, None] == targets[None, :])
        & (slot_order[None, :] < slot_order[:, None])
        & slot_alive[None, :]
    )
    position = jnp.sum(earlier.astype(jnp.int32), axis=1)
    lane_of_slot = jnp.where(slot_alive, targets * per_peer + position, -1)
    lane_ids = jnp.arange(lane_total, dtype=jnp.int32)
    lane_hits = lane_of_slot[None, :] == lane_ids[:, None]
    lane_used = jnp.any(lane_hits, axis=1)
    lane_source = jnp.sum(jnp.where(lane_hits, slot_order[None, :], 0), axis=1)
    lane_place = jnp.where(lane_used, jnp.take(places, lane_source), -1)
    work_ids = jnp.arange(work_count, dtype=jnp.int32)

    def run_couple(couple):
        return correlate(couple, tables)

    outgoing = jnp.take(pair_stack, lane_source, axis=0)
    outgoing = jnp.where(lane_used[:, None, None, None], outgoing, jnp.zeros_like(outgoing))
    arrived, arrived_place = (
        lax.all_to_all(outgoing, "tile", split_axis=0, concat_axis=0, tiled=True),
        lax.all_to_all(lane_place, "tile", split_axis=0, concat_axis=0, tiled=True),
    )
    present, picked = settle(arrived_place, lane_ids, work_ids)
    chosen = jnp.take(arrived, picked, axis=0)
    work_pairs = jnp.where(present[:, None, None, None], chosen, jnp.zeros_like(chosen))
    surfaces = lax.map(run_couple, work_pairs)
    work_peaks = jnp.max(surfaces, axis=(1, 2))
    work_peaks = jnp.where(present, work_peaks, jnp.zeros_like(work_peaks))
    returned = jnp.take(work_peaks, jnp.maximum(arrived_place, 0))
    returned = jnp.where(arrived_place >= 0, returned, jnp.zeros_like(returned))
    homecoming = lax.all_to_all(returned, "tile", split_axis=0, concat_axis=0, tiled=True)
    slot_peaks = jnp.take(homecoming, jnp.maximum(lane_of_slot, 0))
    peak_values = jnp.where(slot_alive, slot_peaks, jnp.zeros_like(slot_peaks))
    return (surfaces[None, None], peak_values[None, None])


def solution(mesh):
    in_specs = (
        P(("groups", "sect"), "tile", "half", None, None),
        P(None, ("groups", "sect"), "tile", "half"),
        P(None, ("groups", "sect"), "tile", "half"),
    )
    out_specs = (
        P(("groups", "sect"), "tile", "half", None, None),
        P(("groups", "sect"), "tile", "half"),
    )
    return jax.shard_map(body, mesh=mesh, in_specs=in_specs, out_specs=out_specs, check_vma=False)
```

profile of v0, /device:TPU:0, one launch (start us, length us, event | category | flops | bytes accessed | tf_op | source)
XLA Modules:
  0.0 304.9 jit_solution(11675553964444325043)
XLA Ops:
  7.2 8.7 %all-to-all-start = ((s32[4,3,1]{1,2,0:T(1,128)}), s32[4,3,1]{1,2,0:T(1,128)S(1)}, u32[]{:S(2)}, u32[]{:S(2)}) async-start(s32[4,3,1]{1,2,0:T(1,128)} %bitcast.4), calls=%async_computation | async-start | bytes 4096 | tf_op jit(solution)/shard_map/all_to_all | solution.py:119
  16.6 2.2 gather_fusion.1
  20.3 31.3 %collective-permute-done = bf16[16,256,256]{2,1,0:T(8,128)(2,1)} collective-permute-done((bf16[16,256,256]{2,1,0:T(8,128)(2,1)}, bf16[16,256,256]{2,1,0:T(8,128)(2,1)}, u32[]{:S(2)}, u32[]{:S(2)}) %collective-permute-start) | collective-permute-done | bytes 2097184 | tf_op jit(solution)/shard_map/ppermute | solution.py:14
  52.2 4.5 %pad_maximum_fusion = bf16[32,256,256]{2,1,0:T(8,128)(2,1)} fusion(bf16[16,256,256]{2,1,0:T(8,128)(2,1)} %collective-permute-done.1, bf16[16,256,256]{2,1,0:T(8,128)(2,1)} %collective-permute-done), kind=kLoop, calls=%fused_computation.136 | loop fusion | flops 2097152 | bytes 8388608 | tf_op jit(solution)/shard_map/concatenate | solution.py:94
  56.7 2.8 gather_fusion.2
  61.2 2.5 gather_fusion.3
  63.7 4.0 %select_select_fusion = bf16[12,2,256,256]{3,2,1,0:T(8,128)(2,1)} fusion(bf16[12,2,256,256]{3,2,1,0:T(8,128)(2,1)} %gather_fusion.3, pred[12]{0:T(512)(128)(4,1)S(1)} %compare_and_fusion.2, pred[12]{0:T(512)(128)(4,1)S(1)} %fusion.139), kind=kLoop, calls=%fused_computation.138 | loop fusion | flops 3145728 | bytes 6291480 | tf_op jit(solution)/shard_map/jit(_where)/select_n | solution.py:116
  67.7 7.9 %all-to-all-start.1 = ((bf16[12,2,256,256]{3,2,1,0:T(8,128)(2,1)}), bf16[12,2,256,256]{3,2,1,0:T(8,128)(2,1)S(1)}, u32[]{:S(2)}, u32[]{:S(2)}) async-start(bf16[12,2,256,256]{3,2,1,0:T(8,128)(2,1)} %select_select_fusion), calls=%async_computation.1 | async-start | bytes 6291456 | tf_op jit(solution)/shard_map/all_to_all | solution.py:118
  76.6 1.6 fusion.138
  78.3 2.0 subtract_convert_fusion
  81.8 63.4 %all-to-all-done.1 = bf16[12,2,256,256]{3,2,1,0:T(8,128)(2,1)S(1)} async-done(((bf16[12,2,256,256]{3,2,1,0:T(8,128)(2,1)}), bf16[12,2,256,256]{3,2,1,0:T(8,128)(2,1)S(1)}, u32[]{:S(2)}, u32[]{:S(2)}) %all-to-all-start.1) | async-done | bytes 3145760 | tf_op jit(solution)/shard_map/all_to_all | solution.py:118
  145.2 1.9 gather_fusion.4
  147.0 1.8 select_select_fusion.1
  148.9 143.3 %while.12 = (s32[]{:T(128)}, f32[6,256,256]{1,2,0:T(8,128)S(1)}, bf16[6,2,256,256]{3,2,1,0:T(8,128)(2,1)S(1)}, bf16[256,256]{1,0:T(8,128)(2,1)S(1)}, bf16[256,25...) while((s32[]{:T(128)}, f32[6,256,256]{1,2,0:T(8,128)S(1)}, ...), condition=%wide.region_6.7_spmd.clone.clone, body=%wide.region_5.6_spmd.clone.clone.sunk | while | flops 1697120256 | bytes 15990933 | solution.py:124
  164.7 1.4 fusion.248
  166.1 1.4 convolution_add_fusion.20
  167.5 1.4 fusion.246
  168.9 1.4 convolution_subtract_fusion.7
  188.5 1.4 fusion.248
  190.0 1.4 convolution_add_fusion.20
  192.8 1.4 convolution_subtract_fusion.7
  212.4 1.4 fusion.248
  216.6 1.4 convolution_subtract_fusion.7
  236.3 1.4 fusion.248
  240.5 1.4 convolution_subtract_fusion.7
  260.2 1.4 fusion.248
  264.4 1.4 convolution_subtract_fusion.7
  284.0 1.4 fusion.248
  288.3 1.4 convolution_subtract_fusion.7
  293.8 3.2 %all-to-all-start.2 = ((f32[4,3,1]{1,2,0:T(1,128)}), f32[4,3,1]{1,2,0:T(1,128)S(1)}, u32[]{:S(2)}, u32[]{:S(2)}) async-start(f32[4,3,1]{1,2,0:T(1,128)} %bitcast.22), calls=%async_computation.2 | async-start | bytes 4096 | tf_op jit(solution)/shard_map/all_to_all | solution.py:129
  297.1 1.6 copy.13
  298.7 3.8 %all-to-all-done.2 = f32[4,3,1]{1,2,0:T(1,128)S(1)} async-done(((f32[4,3,1]{1,2,0:T(1,128)}), f32[4,3,1]{1,2,0:T(1,128)S(1)}, u32[]{:S(2)}, u32[]{:S(2)}) %all-to-all-start.2) | async-done | bytes 80 | tf_op jit(solution)/shard_map/all_to_all | solution.py:129
  (176 shorter events, 138.6 us)
Async XLA Ops:
  0.6 50.9 %collective-permute-start = (bf16[16,256,256]{2,1,0:T(8,128)(2,1)}, bf16[16,256,256]{2,1,0:T(8,128)(2,1)}, u32[]{:S(2)}, u32[]{:S(2)}) collective-permute-start(bf16[16,256,256]{2,1,0:T(8,128)(2,1)} %bitcast.200), channel_id=1, source_target_pairs={{4,0},{8,4},{12,8},{5,1},{9,5},{13,9},{6,2},{10,6},{14,10},{7,3},{... | collective-permute-start | bytes 6291464 | tf_op jit(solution)/shard_map/ppermute | solution.py:14
  1.9 50.2 %collective-permute-start.1 = (bf16[16,256,256]{2,1,0:T(8,128)(2,1)}, bf16[16,256,256]{2,1,0:T(8,128)(2,1)}, u32[]{:S(2)}, u32[]{:S(2)}) collective-permute-start(bf16[16,256,256]{2,1,0:T(8,128)(2,1)} %bitcast.201), channel_id=1, source_target_pairs={{2,0},{3,1},{6,4},{7,5},{10,8},{11,9},{14,12},{15,13},{18,16},{19,... | collective-permute-start | bytes 6291464 | tf_op jit(solution)/shard_map/ppermute | solution.py:14
  7.2 60.5 %all-to-all-start = ((s32[4,3,1]{1,2,0:T(1,128)}), s32[4,3,1]{1,2,0:T(1,128)S(1)}, u32[]{:S(2)}, u32[]{:S(2)}) async-start(s32[4,3,1]{1,2,0:T(1,128)} %bitcast.4), calls=%async_computation | async-start | bytes 4096 | tf_op jit(solution)/shard_map/all_to_all | solution.py:119
  16.6 2.3 copy-start.3
  59.5 1.4 copy-start.1
  67.7 10.6 %copy-start.2 = (s32[2,1,1,12]{3,2,1,0:T(1,128)S(1)}, s32[2,1,1,12]{3,2,1,0:T(1,128)}, u32[]{:S(2)}) copy-start(s32[2,1,1,12]{3,2,1,0:T(1,128)} %param.7) | copy-start | bytes 292
  67.7 77.5 %all-to-all-start.1 = ((bf16[12,2,256,256]{3,2,1,0:T(8,128)(2,1)}), bf16[12,2,256,256]{3,2,1,0:T(8,128)(2,1)S(1)}, u32[]{:S(2)}, u32[]{:S(2)}) async-start(bf16[12,2,256,256]{3,2,1,0:T(8,128)(2,1)} %select_select_fusion), calls=%async_computation.1 | async-start | bytes 6291456 | tf_op jit(solution)/shard_map/all_to_all | solution.py:118
  147.0 1.9 copy-start
  293.8 8.6 %all-to-all-start.2 = ((f32[4,3,1]{1,2,0:T(1,128)}), f32[4,3,1]{1,2,0:T(1,128)S(1)}, u32[]{:S(2)}, u32[]{:S(2)}) async-start(f32[4,3,1]{1,2,0:T(1,128)} %bitcast.22), calls=%async_computation.2 | async-start | bytes 4096 | tf_op jit(solution)/shard_map/all_to_all | solution.py:129
where the time goes:
time: 305 us
  matrix products  142 us (47%)
  waiting for transfers between devices  99.1 us (32%)
  other arithmetic  22.6 us (7%)
  starting transfers between devices  22.5 us (7%)
  local copies, waits for them, and re-layouts  16.6 us (5%)
    dot_general x84, matrix products, matmul(): jnp.dot(left, right, precision=lax.Precision.HIGH, preferred_element_type...  111 us
    all_to_all x1, waiting for transfers between devices, body(): lax.all_to_all(outgoing, 'tile', split_axis=0, concat_axis=0, tiled=True)  63.4 us
    ppermute x2, waiting for transfers between devices, passed_along(): lax.ppermute(value, axis, [(source, source + steps) for source in range(l...  31.9 us
    dot_general x24, matrix products, narrow_product(): jnp.dot(picture, pieces[0], preferred_element_type=jnp.float32)  27 us
    all_to_all x1, starting transfers between devices, body(): lax.all_to_all(lane_place, 'tile', split_axis=0, concat_axis=0, tiled=True)  8.74 us
    all_to_all x1, starting transfers between devices, body(): lax.all_to_all(outgoing, 'tile', split_axis=0, concat_axis=0, tiled=True)  7.94 us
  transfers between devices with their start and end apart: 5, of which 4 were waited for; matrix products, arithmetic and copies ran while one was open for 10% of the time, Pallas kernels for 0%

commit v1 on v0

v1 whole, which is shorter than its diff:
```python
import jax
import jax.numpy as jnp
import numpy as np
from jax import lax
from jax.experimental import pallas as pl
from jax.experimental.pallas import tpu as pltpu
from jax.sharding import PartitionSpec as P

FLOOR = 0.05


def passed_along(value, axis, steps):
    count = lax.axis_size(axis)
    leading, last = (max(0, -steps), min(count, count - steps))
    return lax.ppermute(value, axis, [(source, source + steps) for source in range(leading, last)])


def real_tables(length):
    half = length // 2
    spots = np.arange(length)
    waves = np.arange(half)
    angles = (spots[:, None] * waves[None, :] % length) * (2.0 * np.pi / length)
    sines = np.sin(angles)
    sines[:, 0] = np.cos(np.pi * spots)
    table = np.concatenate([np.cos(angles), sines], axis=1).astype(np.float32)
    upper = table.astype(jnp.bfloat16)
    lower = (table - upper.astype(np.float32)).astype(jnp.bfloat16)
    column = np.stack([upper, lower])
    row = np.stack([upper.T, lower.T])
    return jnp.asarray(column), jnp.asarray(row)


def halves_of(value):
    upper = value.astype(jnp.bfloat16)
    return upper, (value - upper.astype(jnp.float32)).astype(jnp.bfloat16)


def dot(left, right):
    return jnp.dot(left, right, preferred_element_type=jnp.float32)


def left_product(table_ref, value):
    upper, lower = halves_of(value)
    return dot(table_ref[0], upper) + dot(table_ref[0], lower) + dot(table_ref[1], upper)


def right_product(value, table_ref):
    upper, lower = halves_of(value)
    return dot(upper, table_ref[0]) + dot(lower, table_ref[0]) + dot(upper, table_ref[1])


def packed_spectrum(picture, column_ref, row_ref):
    across = dot(picture, column_ref[0]) + dot(picture, column_ref[1])
    return left_product(row_ref, across)


def unpacked(packed, on_row, on_column):
    half = packed.shape[0] // 2
    cc, cs = packed[:half, :half], packed[:half, half:]
    sc, ss = packed[half:, :half], packed[half:, half:]
    edge = on_row | on_column
    plus_re = jnp.where(edge, cc, cc - ss)
    plus_im = jnp.where(on_row, cs, jnp.where(on_column, sc, sc + cs))
    minus_re = jnp.where(on_row, sc, jnp.where(on_column, cs, cc + ss))
    minus_im = jnp.where(edge, ss, cs - sc)
    return (plus_re, plus_im, minus_re, minus_im)


def phases(first_re, first_im, second_re, second_im, floor):
    cross_re = first_re * second_re + first_im * second_im
    cross_im = first_re * second_im - first_im * second_re
    power = cross_re * cross_re + cross_im * cross_im
    factor = jnp.minimum(lax.rsqrt(power), 1.0 / floor)
    return (cross_re * factor, cross_im * factor)


def correlate(first, second, column_ref, row_ref):
    length = first.shape[-1]
    half = length // 2
    floor = FLOOR * length * length
    first_packed = packed_spectrum(first, column_ref, row_ref)
    second_packed = packed_spectrum(second, column_ref, row_ref)
    rows = lax.broadcasted_iota(jnp.int32, (half, half), 0)
    columns = lax.broadcasted_iota(jnp.int32, (half, half), 1)
    on_row, on_column = rows == 0, columns == 0
    corner = on_row & on_column
    one = unpacked(first_packed, on_row, on_column)
    two = unpacked(second_packed, on_row, on_column)
    plus_re, plus_im = phases(one[0], one[1], two[0], two[1], floor)
    minus_re, minus_im = phases(one[2], one[3], two[2], two[3], floor)
    cc = jnp.where(on_row | on_column, plus_re, plus_re + minus_re)
    ss = jnp.where(on_row | on_column, -minus_im, minus_re - plus_re)
    sc = jnp.where(on_row, minus_re, jnp.where(on_column, -plus_im, minus_im - plus_im))
    cs = jnp.where(on_row, -plus_im, jnp.where(on_column, minus_re, -plus_im - minus_im))

    def at_corner(value, top, left):
        product = (
            first_packed[top : top + half, left : left + half]
            * second_packed[top : top + half, left : left + half]
        )
        real = product / jnp.maximum(jnp.abs(product), floor)
        return jnp.where(corner, 0.5 * real, value)

    packed = jnp.concatenate(
        [
            jnp.concatenate([at_corner(cc, 0, 0), at_corner(cs, 0, half)], axis=1),
            jnp.concatenate([at_corner(sc, half, 0), at_corner(ss, half, half)], axis=1),
        ],
        axis=0,
    )
    scale = 2.0 / length
    return left_product(column_ref, right_product(packed * scale, row_ref))


def couple_kernel(picks_ref, first_ref, second_ref, column_ref, row_ref, surface_ref, peak_ref):
    step = pl.program_id(0)

    @pl.when(picks_ref[2, step] == 0)
    def _():
        surface_ref[...] = jnp.zeros_like(surface_ref)
        peak_ref[...] = jnp.zeros_like(peak_ref)

    @pl.when(picks_ref[2, step] != 0)
    def _():
        surface = correlate(first_ref[0, 0], second_ref[0, 0], column_ref, row_ref)
        surface_ref[0] = surface
        peak_ref[...] = jnp.full(peak_ref.shape, jnp.max(surface), jnp.float32)


def correlate_all(picks, first_from, second_from, first_lane, second_lane):
    work_count = picks.shape[1]
    length = first_from.shape[-1]
    column, row = real_tables(length)
    whole_table = pl.BlockSpec((2, length, length), lambda w, p: (0, 0, 0))
    surfaces, peaks = pl.pallas_call(
        couple_kernel,
        grid_spec=pltpu.PrefetchScalarGridSpec(
            num_scalar_prefetch=1,
            grid=(work_count,),
            in_specs=[
                pl.BlockSpec((1, 1, length, length), lambda w, p: (p[0, w], first_lane, 0, 0)),
                pl.BlockSpec((1, 1, length, length), lambda w, p: (p[1, w], second_lane, 0, 0)),
                whole_table,
                whole_table,
            ],
            out_specs=[
                pl.BlockSpec((1, length, length), lambda w, p: (w, 0, 0)),
                pl.BlockSpec((1, 1, 128), lambda w, p: (w, 0, 0)),
            ],
        ),
        out_shape=[
            jax.ShapeDtypeStruct((work_count, length, length), jnp.float32),
            jax.ShapeDtypeStruct((work_count, 1, 128), jnp.float32),
        ],
    )(picks, first_from, second_from, column, row)
    return surfaces, peaks[:, 0, 0]


def settle(arrived_place, lane_ids, work_ids):
    matches = arrived_place[None, :] == work_ids[:, None]
    present = jnp.any(matches, axis=1)
    picked = jnp.sum(jnp.where(matches, lane_ids[None, :], 0), axis=1)
    return (present, picked)


def body(patches, pair_lists, move_plan):
    own_patches = patches[0, 0]
    from_below = passed_along(own_patches, "tile", -1)
    from_next = passed_along(own_patches, "sect", -1)
    pair_kinds = pair_lists[0, 0, 0]
    first_index = pair_lists[1, 0, 0]
    second_index = pair_lists[2, 0, 0]
    targets = move_plan[0, 0, 0]
    places = move_plan[1, 0, 0]
    slot_count = pair_kinds.shape[0]
    patch_count = own_patches.shape[0]
    work_count = slot_count // 2
    tile_count = lax.axis_size("tile")
    per_peer = (slot_count + tile_count - 1) // tile_count
    lane_total = tile_count * per_peer
    slot_alive = targets >= 0
    firsts = jnp.take(own_patches, first_index, axis=0)
    partners = jnp.concatenate([from_below, from_next], axis=0)
    seconds = jnp.take(partners, pair_kinds * patch_count + second_index, axis=0)
    pair_stack = jnp.stack([firsts, seconds], axis=1)
    slot_order = jnp.arange(slot_count, dtype=jnp.int32)
    earlier = (
        (targets[:, None] == targets[None, :])
        & (slot_order[None, :] < slot_order[:, None])
        & slot_alive[None, :]
    )
    position = jnp.sum(earlier.astype(jnp.int32), axis=1)
    lane_of_slot = jnp.where(slot_alive, targets * per_peer + position, -1)
    lane_ids = jnp.arange(lane_total, dtype=jnp.int32)
    lane_hits = lane_of_slot[None, :] == lane_ids[:, None]
    lane_used = jnp.any(lane_hits, axis=1)
    lane_source = jnp.sum(jnp.where(lane_hits, slot_order[None, :], 0), axis=1)
    lane_place = jnp.where(lane_used, jnp.take(places, lane_source), -1)
    work_ids = jnp.arange(work_count, dtype=jnp.int32)
    outgoing = jnp.take(pair_stack, lane_source, axis=0)
    arrived, arrived_place = (
        lax.all_to_all(outgoing, "tile", split_axis=0, concat_axis=0, tiled=True),
        lax.all_to_all(lane_place, "tile", split_axis=0, concat_axis=0, tiled=True),
    )
    present, picked = settle(arrived_place, lane_ids, work_ids)
    picks = jnp.stack([picked, picked, present.astype(jnp.int32)])
    surfaces, work_peaks = correlate_all(picks, arrived, arrived, 0, 1)
    returned = jnp.take(work_peaks, jnp.maximum(arrived_place, 0))
    returned = jnp.where(arrived_place >= 0, returned, jnp.zeros_like(returned))
    homecoming = lax.all_to_all(returned, "tile", split_axis=0, concat_axis=0, tiled=True)
    slot_peaks = jnp.take(homecoming, jnp.maximum(lane_of_slot, 0))
    peak_values = jnp.where(slot_alive, slot_peaks, jnp.zeros_like(slot_peaks))
    return (surfaces[None, None], peak_values[None, None])


def solution(mesh):
    in_specs = (
        P(("groups", "sect"), "tile", "half", None, None),
        P(None, ("groups", "sect"), "tile", "half"),
        P(None, ("groups", "sect"), "tile", "half"),
    )
    out_specs = (
        P(("groups", "sect"), "tile", "half", None, None),
        P(("groups", "sect"), "tile", "half"),
    )
    return jax.shard_map(body, mesh=mesh, in_specs=in_specs, out_specs=out_specs, check_vma=False)
```

time: 305 us -> 174 us (0.57)
  matrix products: 142 us -> 0 us
  Pallas kernels: 0 us -> 13.4 us
  other arithmetic: 22.6 us -> 16.6 us
  waiting for transfers between devices: 99.1 us -> 105 us
    dot_general x132 -> x0, matrix products: 142 us -> none  [the longest x84 111 us: matmul(): jnp.dot(left, right, precision=lax.Precision.HIGH, preferred_element_type...]
    pallas_call x0 -> x1, Pallas kernels: none -> 13.4 us  [correlate_all(): pl.pallas_call(couple_kernel, grid_spec=pltpu.PrefetchScalarGridSpec(num_...]
    convert_element_type x3 -> x1, other arithmetic: 4.59 us -> 0.01 us  [body(): picks = jnp.stack([picked, picked, present.astype(jnp.int32)])]
    all_to_all x1, waiting for transfers between devices: 63.4 us -> 67.3 us  [body(): lax.all_to_all(outgoing, 'tile', split_axis=0, concat_axis=0, tiled=True)]
  transfers between devices with their start and end apart: 5 -> 5, of which waited for: 4 -> 4; matrix products, arithmetic and copies ran while one was open for 10% -> 14% of each run, Pallas kernels for 0% -> 0%
where the time goes in v1:
time: 174 us
  waiting for transfers between devices  105 us (60%)
  starting transfers between devices  22.5 us (13%)
  other arithmetic  16.6 us (10%)
  local copies, waits for them, and re-layouts  15.5 us (9%)
  Pallas kernels  13.4 us (8%)
    all_to_all x1, waiting for transfers between devices, body(): lax.all_to_all(outgoing, 'tile', split_axis=0, concat_axis=0, tiled=True)  67.3 us
    ppermute x2, waiting for transfers between devices, passed_along(): lax.ppermute(value, axis, [(source, source + steps) for source in range(l...  31.9 us
    pallas_call x1, Pallas kernels, correlate_all(): pl.pallas_call(couple_kernel, grid_spec=pltpu.PrefetchScalarGridSpec(num_...  13.4 us
    all_to_all x1, starting transfers between devices, body(): lax.all_to_all(lane_place, 'tile', split_axis=0, concat_axis=0, tiled=True)  8.74 us
    all_to_all x1, starting transfers between devices, body(): lax.all_to_all(outgoing, 'tile', split_axis=0, concat_axis=0, tiled=True)  7.94 us
    all_to_all x1, waiting for transfers between devices, body(): lax.all_to_all(returned, 'tile', split_axis=0, concat_axis=0, tiled=True)  5.37 us
    concatenate x1, other arithmetic, body(): partners = jnp.concatenate([from_below, from_next], axis=0)  4.51 us
    select_n x1, other arithmetic, body(): outgoing = jnp.take(pair_stack, lane_source, axis=0)  3.92 us
  transfers between devices with their start and end apart: 5, of which 4 were waited for; matrix products, arithmetic and copies ran while one was open for 14% of the time, Pallas kernels for 0%

profile of v1, /device:TPU:0, one launch (start us, length us, event | category | flops | bytes accessed | tf_op | source)
XLA Modules:
  0.0 173.5 jit_solution(23973965178806813)
XLA Ops:
  0.6 1.3 collective-permute-start
  1.9 1.3 collective-permute-start.1
  3.2 0.7 slice_bitcast_fusion
  3.9 0.7 broadcast_compare_fusion
  4.8 0.7 add_select_fusion
  5.6 0.7 gather_fusion
  6.6 0.6 select_select_fusion.1
  7.2 8.7 %all-to-all-start = ((s32[4,3,1]{1,2,0:T(1,128)}), s32[4,3,1]{1,2,0:T(1,128)S(1)}, u32[]{:S(2)}, u32[]{:S(2)}) async-start(s32[4,3,1]{1,2,0:T(1,128)} %bitcast.4), calls=%async_computation | async-start | bytes 4096 | tf_op jit(solution)/shard_map/all_to_all | solution.py:203
  15.9 0.7 fusion.7
  16.6 2.2 %gather_fusion.1 = bf16[12,256,256]{2,1,0:T(8,128)(2,1)S(1)} fusion(bf16[16,256,256]{2,1,0:T(8,128)(2,1)} %bitcast.75, s32[1024]{0:T(1024)S(1)} %pad_clamp_fusion.3), kind=kCustom, calls=%fused_computation.1 | custom fusion | bytes 3145776 | tf_op jit(solution)/shard_map/jit(_take)/gather | solution.py:182
  18.9 1.4 bitcast_select_fusion.1
  20.3 31.3 %collective-permute-done = bf16[16,256,256]{2,1,0:T(8,128)(2,1)} collective-permute-done((bf16[16,256,256]{2,1,0:T(8,128)(2,1)}, bf16[16,256,256]{2,1,0:T(8,128)(2,1)}, u32[]{:S(2)}, u32[]{:S(2)}) %collective-permute-start) | collective-permute-done | bytes 2097184 | tf_op jit(solution)/shard_map/ppermute | solution.py:15
  51.5 0.6 collective-permute-done.1
  52.2 4.5 %pad_maximum_fusion = bf16[32,256,256]{2,1,0:T(8,128)(2,1)} fusion(bf16[16,256,256]{2,1,0:T(8,128)(2,1)} %collective-permute-done.1, bf16[16,256,256]{2,1,0:T(8,128)(2,1)} %collective-permute-done), kind=kLoop, calls=%fused_computation.6 | loop fusion | flops 2097152 | bytes 8388608 | tf_op jit(solution)/shard_map/concatenate | solution.py:183
  56.7 2.8 %gather_fusion.2 = bf16[12,256,256]{2,1,0:T(8,128)(2,1)S(1)} fusion(bf16[32,256,256]{2,1,0:T(8,128)(2,1)} %pad_maximum_fusion, s32[1024]{0:T(1024)S(1)} %pad_clamp_fusion.2), kind=kCustom, calls=%fused_computation.2 | custom fusion | bytes 3145776 | tf_op jit(solution)/shard_map/jit(_take)/gather | solution.py:184
  59.8 1.2 copy-done.1
  61.2 2.5 %gather_fusion.3 = bf16[12,2,256,256]{3,2,1,0:T(8,128)(2,1)} fusion(bf16[12,2,256,256]{3,2,0,1:T(8,128)(2,1)S(1)} %pad_maximum_fusion.1, s32[1024]{0:T(1024)S(1)} %pad_clamp_fusion.4), kind=kCustom, calls=%fused_computation.3 | custom fusion | bytes 6291504 | tf_op jit(solution)/shard_map/jit(_take)/gather | solution.py:200
  63.8 3.9 %broadcast_select_fusion = bf16[12,2,256,256]{3,2,1,0:T(8,128)(2,1)} fusion(bf16[12,2,256,256]{3,2,1,0:T(8,128)(2,1)} %gather_fusion.3, pred[12]{0:T(512)(128)(4,1)S(1)} %compare_and_fusion.2), kind=kLoop, calls=%fused_computation.8 | loop fusion | flops 1572864 | bytes 6291468 | tf_op jit(solution)/shard_map/jit(_take)/select_n | solution.py:200
  67.7 7.9 %all-to-all-start.1 = ((bf16[12,2,256,256]{3,2,1,0:T(8,128)(2,1)}), bf16[12,2,256,256]{3,2,1,0:T(8,128)(2,1)S(1)}, u32[]{:S(2)}, u32[]{:S(2)}) async-start(bf16[12,2,256,256]{3,2,1,0:T(8,128)(2,1)} %broadcast_select_fusion), calls=%async_computation.1 | async-start | bytes 6291456 | tf_op jit(solution)/shard_map/all_to_all | solution.py:202
  76.1 0.7 reduce.8
  77.2 0.6 pad_add_fusion.picks_ref
  77.8 67.3 %all-to-all-done.1.first_ref.second_ref = bf16[12,2,256,256]{3,2,1,0:T(8,128)(2,1)S(1)} async-done(((bf16[12,2,256,256]{3,2,1,0:T(8,128)(2,1)}), bf16[12,2,256,256]{3,2,1,0:T(8,128)(2,1)S(1)}, u32[]{:S(2)}, u32[]{:S(2)}) %all-to-all-start.1) | async-done | bytes 3145760 | tf_op jit(solution)/shard_map/all_to_all | solution.py:202
  145.1 1.7 copy-done
  146.8 13.4 %shard_map.68 = (f32[6,256,256]{2,1,0:T(8,128)}, f32[6,1,128]{2,1,0:T(1,128)}) custom-call(s32[3,6]{1,0:T(4,128)} %pad_add_fusion.picks_ref, bf16[12,2,256,256]{3,2,1,0:T(8,128)(2,1)} %copy-done, bf16[12,2,256,256]{3,2,1,0:T(8,128)(2,1)} %copy-done, bf16[2,256,256]{2,1,0:T(8,128)(2,1)} %constant.102.clone.column_ref, ...), custom_call_target="tpu_custom_call" | custom-call | tf_op jit(solution)/shard_map/pallas_call | solution.py:135
  160.3 0.8 slice_reduce_fusion
  161.1 0.7 gather_fusion.4
  161.8 0.6 select_select_fusion
  162.4 3.2 %all-to-all-start.2 = ((f32[4,3,1]{1,2,0:T(1,128)}), f32[4,3,1]{1,2,0:T(1,128)S(1)}, u32[]{:S(2)}, u32[]{:S(2)}) async-start(f32[4,3,1]{1,2,0:T(1,128)} %bitcast.21), calls=%async_computation.2 | async-start | bytes 4096 | tf_op jit(solution)/shard_map/all_to_all | solution.py:210
  165.7 5.4 %all-to-all-done.2 = f32[4,3,1]{1,2,0:T(1,128)S(1)} async-done(((f32[4,3,1]{1,2,0:T(1,128)}), f32[4,3,1]{1,2,0:T(1,128)S(1)}, u32[]{:S(2)}, u32[]{:S(2)}) %all-to-all-start.2) | async-done | bytes 80 | tf_op jit(solution)/shard_map/all_to_all | solution.py:210
  171.6 0.7 reduce.9
  172.3 0.7 gather_fusion.5
  173.0 0.5 bitcast_select_fusion.3
  (35 shorter events, 2.9 us)
Async XLA Ops:
  0.6 18.2 %copy-start.3 = (s32[3,1,1,12]{3,2,1,0:T(1,128)S(1)}, s32[3,1,1,12]{3,2,1,0:T(1,128)}, u32[]{:S(2)}) copy-start(s32[3,1,1,12]{3,2,1,0:T(1,128)} %param.6) | copy-start | bytes 436
  0.6 50.9 %collective-permute-start = (bf16[16,256,256]{2,1,0:T(8,128)(2,1)}, bf16[16,256,256]{2,1,0:T(8,128)(2,1)}, u32[]{:S(2)}, u32[]{:S(2)}) collective-permute-start(bf16[16,256,256]{2,1,0:T(8,128)(2,1)} %bitcast.73), channel_id=1, source_target_pairs={{4,0},{8,4},{12,8},{5,1},{9,5},{13,9},{6,2},{10,6},{14,10},{7,3},{... | collective-permute-start | bytes 6291464 | tf_op jit(solution)/shard_map/ppermute | solution.py:15
  1.9 50.2 %collective-permute-start.1 = (bf16[16,256,256]{2,1,0:T(8,128)(2,1)}, bf16[16,256,256]{2,1,0:T(8,128)(2,1)}, u32[]{:S(2)}, u32[]{:S(2)}) collective-permute-start(bf16[16,256,256]{2,1,0:T(8,128)(2,1)} %bitcast.74), channel_id=1, source_target_pairs={{2,0},{3,1},{6,4},{7,5},{10,8},{11,9},{14,12},{15,13},{18,16},{19,... | collective-permute-start | bytes 6291464 | tf_op jit(solution)/shard_map/ppermute | solution.py:15
  7.2 60.5 %all-to-all-start = ((s32[4,3,1]{1,2,0:T(1,128)}), s32[4,3,1]{1,2,0:T(1,128)S(1)}, u32[]{:S(2)}, u32[]{:S(2)}) async-start(s32[4,3,1]{1,2,0:T(1,128)} %bitcast.4), calls=%async_computation | async-start | bytes 4096 | tf_op jit(solution)/shard_map/all_to_all | solution.py:203
  59.5 1.4 copy-start.1
  67.7 7.9 %copy-start.2 = (s32[2,1,1,12]{3,2,1,0:T(1,128)S(1)}, s32[2,1,1,12]{3,2,1,0:T(1,128)}, u32[]{:S(2)}) copy-start(s32[2,1,1,12]{3,2,1,0:T(1,128)} %param.7) | copy-start | bytes 292
  67.7 77.5 %all-to-all-start.1 = ((bf16[12,2,256,256]{3,2,1,0:T(8,128)(2,1)}), bf16[12,2,256,256]{3,2,1,0:T(8,128)(2,1)S(1)}, u32[]{:S(2)}, u32[]{:S(2)}) async-start(bf16[12,2,256,256]{3,2,1,0:T(8,128)(2,1)} %broadcast_select_fusion), calls=%async_computation.1 | async-start | bytes 6291456 | tf_op jit(solution)/shard_map/all_to_all | solution.py:202
  145.1 1.7 copy-start
  162.4 8.6 %all-to-all-start.2 = ((f32[4,3,1]{1,2,0:T(1,128)}), f32[4,3,1]{1,2,0:T(1,128)S(1)}, u32[]{:S(2)}, u32[]{:S(2)}) async-start(f32[4,3,1]{1,2,0:T(1,128)} %bitcast.21), calls=%async_computation.2 | async-start | bytes 4096 | tf_op jit(solution)/shard_map/all_to_all | solution.py:210

commit v2 on v1

v2 whole, which is shorter than its diff:
```python
import functools

import jax
import jax.numpy as jnp
import numpy as np
from jax import lax
from jax.experimental import pallas as pl
from jax.experimental.pallas import tpu as pltpu
from jax.sharding import PartitionSpec as P

FLOOR = 0.05
STEPS = 32767.0
SMALLEST = 1.2e-34
MESH = pl.DeviceIdType.MESH


def real_tables(length):
    half = length // 2
    spots = np.arange(length)
    waves = np.arange(half)
    angles = (spots[:, None] * waves[None, :] % length) * (2.0 * np.pi / length)
    sines = np.sin(angles)
    sines[:, 0] = np.cos(np.pi * spots)
    table = np.concatenate([np.cos(angles), sines], axis=1).astype(np.float32)
    upper = table.astype(jnp.bfloat16)
    lower = (table - upper.astype(np.float32)).astype(jnp.bfloat16)
    column = np.stack([upper, lower])
    row = np.stack([upper.T, lower.T])
    return jnp.asarray(column), jnp.asarray(row)


def halves_of(value):
    upper = value.astype(jnp.bfloat16)
    return upper, (value - upper.astype(jnp.float32)).astype(jnp.bfloat16)


def dot(left, right):
    return jnp.dot(left, right, preferred_element_type=jnp.float32)


def left_product(table_ref, value):
    upper, lower = halves_of(value)
    return dot(table_ref[0], upper) + dot(table_ref[0], lower) + dot(table_ref[1], upper)


def right_product(value, table_ref):
    upper, lower = halves_of(value)
    return dot(upper, table_ref[0]) + dot(lower, table_ref[0]) + dot(upper, table_ref[1])


def packed_spectrum(picture, column_ref, row_ref):
    across = dot(picture, column_ref[0]) + dot(picture, column_ref[1])
    return left_product(row_ref, across)


def unpacked(packed, on_row, on_column):
    half = packed.shape[0] // 2
    cc, cs = packed[:half, :half], packed[:half, half:]
    sc, ss = packed[half:, :half], packed[half:, half:]
    edge = on_row | on_column
    plus_re = jnp.where(edge, cc, cc - ss)
    plus_im = jnp.where(on_row, cs, jnp.where(on_column, sc, sc + cs))
    minus_re = jnp.where(on_row, sc, jnp.where(on_column, cs, cc + ss))
    minus_im = jnp.where(edge, ss, cs - sc)
    return (plus_re, plus_im, minus_re, minus_im)


def phases(first_re, first_im, second_re, second_im, floor):
    cross_re = first_re * second_re + first_im * second_im
    cross_im = first_re * second_im - first_im * second_re
    power = cross_re * cross_re + cross_im * cross_im
    factor = jnp.minimum(lax.rsqrt(power), 1.0 / floor)
    return (cross_re * factor, cross_im * factor)


def correlate(first, second, column_ref, row_ref):
    length = first.shape[-1]
    half = length // 2
    floor = FLOOR * length * length
    first_packed = packed_spectrum(first, column_ref, row_ref)
    second_packed = packed_spectrum(second, column_ref, row_ref)
    rows = lax.broadcasted_iota(jnp.int32, (half, half), 0)
    columns = lax.broadcasted_iota(jnp.int32, (half, half), 1)
    on_row, on_column = rows == 0, columns == 0
    corner = on_row & on_column
    one = unpacked(first_packed, on_row, on_column)
    two = unpacked(second_packed, on_row, on_column)
    plus_re, plus_im = phases(one[0], one[1], two[0], two[1], floor)
    minus_re, minus_im = phases(one[2], one[3], two[2], two[3], floor)
    cc = jnp.where(on_row | on_column, plus_re, plus_re + minus_re)
    ss = jnp.where(on_row | on_column, -minus_im, minus_re - plus_re)
    sc = jnp.where(on_row, minus_re, jnp.where(on_column, -plus_im, minus_im - plus_im))
    cs = jnp.where(on_row, -plus_im, jnp.where(on_column, minus_re, -plus_im - minus_im))

    def at_corner(value, top, left):
        product = (
            first_packed[top : top + half, left : left + half]
            * second_packed[top : top + half, left : left + half]
        )
        real = product / jnp.maximum(jnp.abs(product), floor)
        return jnp.where(corner, 0.5 * real, value)

    packed = jnp.concatenate(
        [
            jnp.concatenate([at_corner(cc, 0, 0), at_corner(cs, 0, half)], axis=1),
            jnp.concatenate([at_corner(sc, half, 0), at_corner(ss, half, half)], axis=1),
        ],
        axis=0,
    )
    scale = 2.0 / length
    return left_product(column_ref, right_product(packed * scale, row_ref))


def rows_of(lists_ref, plan_ref, slots, target, position):
    def look(slot, carried):
        seen, chosen, used = carried
        hit = (plan_ref[0, 0, 0, slot] == target).astype(jnp.int32)
        match = hit * (seen == position).astype(jnp.int32)
        return (seen + hit, chosen + match * slot, used + match)

    zero = jnp.int32(0)
    _, chosen, used = lax.fori_loop(0, slots, look, (zero, zero, zero), unroll=True)
    return chosen, used


def stitch_kernel(
    sizes,
    lists_ref,
    plan_ref,
    own_ref,
    column_ref,
    row_ref,
    surface_ref,
    peak_ref,
    below_ref,
    next_ref,
    sent_ref,
    sent_note_ref,
    got_ref,
    got_note_ref,
    fetch_send,
    fetch_recv,
    code_send,
    code_recv,
    note_send,
    note_recv,
):
    tiles, sections, per_peer, slots, works = sizes
    tile, sect = lax.axis_index("tile"), lax.axis_index("sect")
    lanes = tiles * per_peer

    barrier = pltpu.get_barrier_semaphore()
    for shift in range(1, tiles):
        pl.semaphore_signal(
            barrier, inc=1, device_id={"tile": lax.rem(tile + shift, tiles)}, device_id_type=MESH
        )

    @pl.when(sect > 0)
    def _():
        pl.semaphore_signal(barrier, inc=1, device_id={"sect": sect - 1}, device_id_type=MESH)

    @pl.when(sect < sections - 1)
    def _():
        pl.semaphore_signal(barrier, inc=1, device_id={"sect": sect + 1}, device_id_type=MESH)

    neighbours = lax.min(sect, 1) + lax.min(sections - 1 - sect, 1)
    pl.semaphore_wait(barrier, tiles - 1 + neighbours)

    def fetch(axis, place, target_ref, index):
        return pltpu.make_async_remote_copy(
            src_ref=own_ref.at[0, 0],
            dst_ref=target_ref,
            send_sem=fetch_send.at[index],
            recv_sem=fetch_recv.at[index],
            device_id={axis: place},
            device_id_type=MESH,
        )

    to_above = fetch("tile", lax.max(tile - 1, 0), below_ref, 0)
    to_before = fetch("sect", lax.max(sect - 1, 0), next_ref, 1)

    @pl.when(tile > 0)
    def _():
        to_above.start()

    @pl.when(sect > 0)
    def _():
        to_before.start()

    surface_ref[...] = jnp.zeros_like(surface_ref)
    peak_ref[...] = jnp.zeros_like(peak_ref)

    @pl.when(tile < tiles - 1)
    def _():
        to_above.wait_recv()

    @pl.when(sect < sections - 1)
    def _():
        to_before.wait_recv()

    def copies(lane, target):
        code = pltpu.make_async_remote_copy(
            src_ref=sent_ref.at[lane],
            dst_ref=got_ref.at[lane],
            send_sem=code_send.at[lane],
            recv_sem=code_recv.at[lane],
            device_id={"tile": target},
            device_id_type=MESH,
        )
        note = pltpu.make_async_remote_copy(
            src_ref=sent_note_ref.at[lane],
            dst_ref=got_note_ref.at[lane],
            send_sem=note_send.at[lane],
            recv_sem=note_recv.at[lane],
            device_id={"tile": target},
            device_id_type=MESH,
        )
        return code, note

    slot_ids = lax.broadcasted_iota(jnp.int32, peak_ref.shape, 1)

    def settle(code, note):
        found = code.astype(jnp.int32).astype(jnp.float32) * note[0:1]
        place = note[1:2]
        for work in range(works):
            surface_ref[0, 0, work] = jnp.where(
                place == float(work), found, surface_ref[0, 0, work]
            )

    def correlate_lane(lane, carried):
        shift = tiles - 1 - lane // per_peer
        target = lax.rem(tile + shift, tiles)
        slot, used = rows_of(lists_ref, plan_ref, slots, target, lax.rem(lane, per_peer))
        kind = lists_ref[0, 0, 0, slot]
        first = own_ref[0, 0, lists_ref[1, 0, 0, slot]]
        other = lists_ref[2, 0, 0, slot]
        second = jnp.where(kind == 0, below_ref[other], next_ref[other])
        surface = correlate(first, second, column_ref, row_ref)
        peak = jnp.max(surface)
        peak_ref[...] = jnp.where(
            (slot_ids == slot) & (used > 0), jnp.full(peak_ref.shape, peak), peak_ref[...]
        )
        place = jnp.where(used > 0, plan_ref[1, 0, 0, slot], -1).astype(jnp.float32)
        tallest = jnp.max(jnp.abs(surface), axis=0, keepdims=True)
        tallest = jnp.maximum(tallest, SMALLEST)
        code = jnp.round(surface * (STEPS / tallest)).astype(jnp.int32).astype(jnp.int16)
        sent_ref[lane] = code
        note_row = lax.broadcasted_iota(jnp.int32, sent_note_ref.shape[1:], 0)
        sent_note_ref[lane] = jnp.where(note_row == 0, tallest * (1.0 / STEPS), place)

        @pl.when(shift > 0)
        def _():
            code_copy, note_copy = copies(lane, target)
            note_copy.start()
            code_copy.start()

        return carried

    lax.fori_loop(0, lanes, correlate_lane, 0)

    def settle_own(lane, carried):
        settle(sent_ref[lane], sent_note_ref[lane])
        return carried

    lax.fori_loop(lanes - per_peer, lanes, settle_own, 0)

    def settle_lane(lane, carried):
        code_copy, note_copy = copies(lane, lax.rem(tile + tiles - 1 - lane // per_peer, tiles))
        note_copy.wait()
        code_copy.wait()
        settle(got_ref[lane], got_note_ref[lane])
        return carried

    lax.fori_loop(0, lanes - per_peer, settle_lane, 0)

    @pl.when(tile > 0)
    def _():
        to_above.wait_send()

    @pl.when(sect > 0)
    def _():
        to_before.wait_send()


def body(patches, pair_lists, move_plan):
    length = patches.shape[-1]
    slots = pair_lists.shape[-1]
    works = slots // 2
    tiles, sections = lax.axis_size("tile"), lax.axis_size("sect")
    per_peer = (slots + tiles - 1) // tiles
    lanes = tiles * per_peer
    column, row = real_tables(length)
    vmem = pl.BlockSpec(memory_space=pltpu.VMEM)
    smem = pl.BlockSpec(memory_space=pltpu.SMEM)
    surfaces, peaks = pl.pallas_call(
        functools.partial(stitch_kernel, (tiles, sections, per_peer, slots, works)),
        in_specs=[smem, smem, vmem, vmem, vmem],
        out_specs=[vmem, vmem],
        out_shape=[
            jax.ShapeDtypeStruct((1, 1, works, length, length), jnp.float32),
            jax.ShapeDtypeStruct((1, 128), jnp.float32),
        ],
        scratch_shapes=[
            pltpu.VMEM(patches.shape[2:], jnp.bfloat16),
            pltpu.VMEM(patches.shape[2:], jnp.bfloat16),
            pltpu.VMEM((lanes, length, length), jnp.int16),
            pltpu.VMEM((lanes, 8, length), jnp.float32),
            pltpu.VMEM((lanes, length, length), jnp.int16),
            pltpu.VMEM((lanes, 8, length), jnp.float32),
            pltpu.SemaphoreType.DMA((2,)),
            pltpu.SemaphoreType.DMA((2,)),
            pltpu.SemaphoreType.DMA((lanes,)),
            pltpu.SemaphoreType.DMA((lanes,)),
            pltpu.SemaphoreType.DMA((lanes,)),
            pltpu.SemaphoreType.DMA((lanes,)),
        ],
        compiler_params=pltpu.CompilerParams(collective_id=0, has_side_effects=True),
    )(pair_lists, move_plan, patches, column, row)
    return (surfaces, peaks[:, None, :slots])


def solution(mesh):
    in_specs = (
        P(("groups", "sect"), "tile", "half", None, None),
        P(None, ("groups", "sect"), "tile", "half"),
        P(None, ("groups", "sect"), "tile", "half"),
    )
    out_specs = (
        P(("groups", "sect"), "tile", "half", None, None),
        P(("groups", "sect"), "tile", "half"),
    )
    return jax.shard_map(body, mesh=mesh, in_specs=in_specs, out_specs=out_specs, check_vma=False)
```

time: 174 us -> 98.8 us (0.57)
  waiting for transfers between devices: 105 us -> 0 us
  Pallas kernels: 13.4 us -> 94.1 us
  starting transfers between devices: 22.5 us -> 0 us
  other arithmetic: 16.6 us -> 0 us
  local copies, waits for them, and re-layouts: 15.5 us -> 3.92 us
    pallas_call x1, Pallas kernels: 13.4 us -> 94.1 us  [body(): pl.pallas_call(functools.partial(stitch_kernel, (tiles, sections, per_pee...]
    all_to_all x3 -> x0, waiting for transfers between devices: 72.7 us -> none  [the longest x1 67.3 us: body(): lax.all_to_all(outgoing, 'tile', split_axis=0, concat_axis=0, tiled=True)]
    ppermute x2 -> x0, waiting for transfers between devices: 31.9 us -> none  [passed_along(): lax.ppermute(value, axis, [(source, source + steps) for source in range(l...]
    all_to_all x3 -> x0, starting transfers between devices: 19.9 us -> none  [the longest x1 8.74 us: body(): lax.all_to_all(lane_place, 'tile', split_axis=0, concat_axis=0, tiled=True)]
    gather x8 -> x0, local copies, waits for them, and re-layouts: 9.73 us -> none  [the longest x1 2.83 us: body(): jnp.take(partners, pair_kinds * patch_count + second_index, axis=0)]
    select_n x10 -> x0, other arithmetic: 8.54 us -> none  [the longest x1 3.92 us: body(): outgoing = jnp.take(pair_stack, lane_source, axis=0)]
    concatenate x1 -> x0, other arithmetic: 4.51 us -> none  [body(): partners = jnp.concatenate([from_below, from_next], axis=0)]
    ppermute x2 -> x0, starting transfers between devices: 2.58 us -> none  [passed_along(): lax.ppermute(value, axis, [(source, source + steps) for source in range(l...]
  transfers between devices with their start and end apart: 5 -> 0, of which waited for: 4 -> 0; matrix products, arithmetic and copies ran while one was open for 14% -> 0% of each run, Pallas kernels for 0% -> 0%
where the time goes in v2:
time: 98.8 us; the launch traced here: 98.7 us
  Pallas kernels  94.1 us (95%)
  local copies, waits for them, and re-layouts  3.92 us (4%)
    pallas_call x1, Pallas kernels, body(): pl.pallas_call(functools.partial(stitch_kernel, (tiles, sections, per_pee...  94.1 us
    unnamed x1, local copies, waits for them, and re-layouts  2.73 us

profile of v2, /device:TPU:0, one launch (start us, length us, event | category | flops | bytes accessed | tf_op | source)
XLA Modules:
  0.0 98.7 jit_solution(5513392051600350345)
XLA Ops:
  0.6 94.1 %shard_map.68 = (f32[1,1,6,256,256]{4,3,2,1,0:T(8,128)}, f32[1,128]{1,0:T(1,128)}) custom-call(s32[3,1,1,12]{3,2,1,0:T(1,128)} %lists_ref.1, s32[2,1,1,12]{3,2,1,0:T(1,128)} %plan_ref.1, bf16[1,1,16,256,256]{4,3,2,1,0:T(8,128)(2,1)} %own_ref.1, bf16[2,256,256]{2,1,0:T(8,128)(2,1)} %constant.4.clone.column_ref, bf16[2,256,256]{2,1,0:T(8,128)(2,1)} %constant.5.clone.row_ref), custom_call_target="tpu_custom_call" | custom-call | tf_op jit(solution)/shard_map/pallas_call | solution.py:295
  94.7 1.2 %slice_bitcast_fusion = f32[1,1,12]{2,1,0:T(1,128)} fusion(f32[1,128]{1,0:T(1,128)} %get-tuple-element.5), kind=kLoop, calls=%fused_computation | loop fusion | bytes 96 | tf_op jit(solution)/shard_map/broadcast_in_dim | solution.py:319
  95.9 2.7 %copy.8 = f32[1,1,6,256,256]{4,3,2,1,0:T(8,128)} copy(f32[1,1,6,256,256]{4,3,2,1,0:T(8,128)} %get-tuple-element.8) | data formatting | bytes 3145728

commit v3 on v2

--- a/solution.py
+++ b/solution.py
@@ -111,27 +111,36 @@
     return left_product(column_ref, right_product(packed * scale, row_ref))
 
 
-def rows_of(lists_ref, plan_ref, slots, target, position):
+def passed_on(value, axis):
+    count = lax.axis_size(axis)
+    return lax.ppermute(value, axis, [(source, source + 1) for source in range(count - 1)])
+
+
+def slot_of(table_ref, target, position):
     def look(slot, carried):
         seen, chosen, used = carried
-        hit = (plan_ref[0, 0, 0, slot] == target).astype(jnp.int32)
+        hit = (table_ref[3, 0, 0, slot] == target).astype(jnp.int32)
         match = hit * (seen == position).astype(jnp.int32)
         return (seen + hit, chosen + match * slot, used + match)
 
     zero = jnp.int32(0)
+    slots = table_ref.shape[-1]
     _, chosen, used = lax.fori_loop(0, slots, look, (zero, zero, zero), unroll=True)
     return chosen, used
 
 
 def stitch_kernel(
     sizes,
-    lists_ref,
-    plan_ref,
+    table_ref,
+    above_table_ref,
+    before_table_ref,
     own_ref,
     column_ref,
     row_ref,
     surface_ref,
     peak_ref,
+    to_above_ref,
+    to_before_ref,
     below_ref,
     next_ref,
     sent_ref,
@@ -145,7 +154,7 @@
     note_send,
     note_recv,
 ):
-    tiles, sections, per_peer, slots, works = sizes
+    tiles, sections, per_peer, works = sizes
     tile, sect = lax.axis_index("tile"), lax.axis_index("sect")
     lanes = tiles * per_peer
 
@@ -166,37 +175,53 @@
     neighbours = lax.min(sect, 1) + lax.min(sections - 1 - sect, 1)
     pl.semaphore_wait(barrier, tiles - 1 + neighbours)
 
-    def fetch(axis, place, target_ref, index):
+    def target_of(owner_tile, lane):
+        return lax.rem(owner_tile + tiles - 1 - lane // per_peer, tiles)
+
+    def stage(lane, carried):
+        position = lax.rem(lane, per_peer)
+        slot, _ = slot_of(above_table_ref, target_of(tile + tiles - 1, lane), position)
+        to_above_ref[lane] = own_ref[0, 0, above_table_ref[2, 0, 0, slot]]
+        slot, _ = slot_of(before_table_ref, target_of(tile, lane), position)
+        to_before_ref[lane] = own_ref[0, 0, before_table_ref[2, 0, 0, slot]]
+        return carried
+
+    lax.fori_loop(0, lanes, stage, 0)
+
+    def to_above(lane):
         return pltpu.make_async_remote_copy(
-            src_ref=own_ref.at[0, 0],
-            dst_ref=target_ref,
-            send_sem=fetch_send.at[index],
-            recv_sem=fetch_recv.at[index],
-            device_id={axis: place},
+            src_ref=to_above_ref.at[lane],
+            dst_ref=below_ref.at[lane],
+            send_sem=fetch_send.at[0, lane],
+            recv_sem=fetch_recv.at[0, lane],
+            device_id={"tile": lax.max(tile - 1, 0)},
             device_id_type=MESH,
         )
 
-    to_above = fetch("tile", lax.max(tile - 1, 0), below_ref, 0)
-    to_before = fetch("sect", lax.max(sect - 1, 0), next_ref, 1)
-
-    @pl.when(tile > 0)
-    def _():
-        to_above.start()
-
-    @pl.when(sect > 0)
-    def _():
-        to_before.start()
-
+    def to_before(lane):
+        return pltpu.make_async_remote_copy(
+            src_ref=to_before_ref.at[lane],
+            dst_ref=next_ref.at[lane],
+            send_sem=fetch_send.at[1, lane],
+            recv_sem=fetch_recv.at[1, lane],
+            device_id={"sect": lax.max(sect - 1, 0)},
+            device_id_type=MESH,
+        )
+
+    def send_patches(lane, carried):
+        @pl.when(tile > 0)
+        def _():
+            to_above(lane).start()
+
+        @pl.when(sect > 0)
+        def _():
+            to_before(lane).start()
+
+        return carried
+
+    lax.fori_loop(0, lanes, send_patches, 0)
     surface_ref[...] = jnp.zeros_like(surface_ref)
     peak_ref[...] = jnp.zeros_like(peak_ref)
-
-    @pl.when(tile < tiles - 1)
-    def _():
-        to_above.wait_recv()
-
-    @pl.when(sect < sections - 1)
-    def _():
-        to_before.wait_recv()
 
     def copies(lane, target):
         code = pltpu.make_async_remote_copy(
@@ -229,18 +254,26 @@
 
     def correlate_lane(lane, carried):
         shift = tiles - 1 - lane // per_peer
-        target = lax.rem(tile + shift, tiles)
-        slot, used = rows_of(lists_ref, plan_ref, slots, target, lax.rem(lane, per_peer))
-        kind = lists_ref[0, 0, 0, slot]
-        first = own_ref[0, 0, lists_ref[1, 0, 0, slot]]
-        other = lists_ref[2, 0, 0, slot]
-        second = jnp.where(kind == 0, below_ref[other], next_ref[other])
+        target = target_of(tile, lane)
+        slot, used = slot_of(table_ref, target, lax.rem(lane, per_peer))
+        kind = table_ref[0, 0, 0, slot]
+        first = own_ref[0, 0, table_ref[1, 0, 0, slot]]
+
+        @pl.when(tile < tiles - 1)
+        def _():
+            to_above(lane).wait_recv()
+
+        @pl.when(sect < sections - 1)
+        def _():
+            to_before(lane).wait_recv()
+
+        second = jnp.where(kind == 0, below_ref[lane], next_ref[lane])
         surface = correlate(first, second, column_ref, row_ref)
         peak = jnp.max(surface)
         peak_ref[...] = jnp.where(
             (slot_ids == slot) & (used > 0), jnp.full(peak_ref.shape, peak), peak_ref[...]
         )
-        place = jnp.where(used > 0, plan_ref[1, 0, 0, slot], -1).astype(jnp.float32)
+        place = jnp.where(used > 0, table_ref[4, 0, 0, slot], -1).astype(jnp.float32)
         tallest = jnp.max(jnp.abs(surface), axis=0, keepdims=True)
         tallest = jnp.maximum(tallest, SMALLEST)
         code = jnp.round(surface * (STEPS / tallest)).astype(jnp.int32).astype(jnp.int16)
@@ -265,7 +298,7 @@
     lax.fori_loop(lanes - per_peer, lanes, settle_own, 0)
 
     def settle_lane(lane, carried):
-        code_copy, note_copy = copies(lane, lax.rem(tile + tiles - 1 - lane // per_peer, tiles))
+        code_copy, note_copy = copies(lane, target_of(tile, lane))
         note_copy.wait()
         code_copy.wait()
         settle(got_ref[lane], got_note_ref[lane])
@@ -273,13 +306,18 @@
 
     lax.fori_loop(0, lanes - per_peer, settle_lane, 0)
 
-    @pl.when(tile > 0)
-    def _():
-        to_above.wait_send()
-
-    @pl.when(sect > 0)
-    def _():
-        to_before.wait_send()
+    def patches_left(lane, carried):
+        @pl.when(tile > 0)
+        def _():
+            to_above(lane).wait_send()
+
+        @pl.when(sect > 0)
+        def _():
+            to_before(lane).wait_send()
+
+        return carried
+
+    lax.fori_loop(0, lanes, patches_left, 0)
 
 
 def body(patches, pair_lists, move_plan):
@@ -290,32 +328,36 @@
     per_peer = (slots + tiles - 1) // tiles
     lanes = tiles * per_peer
     column, row = real_tables(length)
+    table = jnp.concatenate([pair_lists, move_plan], axis=0)
+    above_table, before_table = passed_on(table, "tile"), passed_on(table, "sect")
     vmem = pl.BlockSpec(memory_space=pltpu.VMEM)
     smem = pl.BlockSpec(memory_space=pltpu.SMEM)
     surfaces, peaks = pl.pallas_call(
-        functools.partial(stitch_kernel, (tiles, sections, per_peer, slots, works)),
-        in_specs=[smem, smem, vmem, vmem, vmem],
+        functools.partial(stitch_kernel, (tiles, sections, per_peer, works)),
+        in_specs=[smem, smem, smem, vmem, vmem, vmem],
         out_specs=[vmem, vmem],
         out_shape=[
             jax.ShapeDtypeStruct((1, 1, works, length, length), jnp.float32),
             jax.ShapeDtypeStruct((1, 128), jnp.float32),
         ],
         scratch_shapes=[
-            pltpu.VMEM(patches.shape[2:], jnp.bfloat16),
-            pltpu.VMEM(patches.shape[2:], jnp.bfloat16),
+            pltpu.VMEM((lanes, length, length), jnp.bfloat16),
+            pltpu.VMEM((lanes, length, length), jnp.bfloat16),
+            pltpu.VMEM((lanes, length, length), jnp.bfloat16),
+            pltpu.VMEM((lanes, length, length), jnp.bfloat16),
             pltpu.VMEM((lanes, length, length), jnp.int16),
             pltpu.VMEM((lanes, 8, length), jnp.float32),
             pltpu.VMEM((lanes, length, length), jnp.int16),
             pltpu.VMEM((lanes, 8, length), jnp.float32),
-            pltpu.SemaphoreType.DMA((2,)),
-            pltpu.SemaphoreType.DMA((2,)),
+            pltpu.SemaphoreType.DMA((2, lanes)),
+            pltpu.SemaphoreType.DMA((2, lanes)),
             pltpu.SemaphoreType.DMA((lanes,)),
             pltpu.SemaphoreType.DMA((lanes,)),
             pltpu.SemaphoreType.DMA((lanes,)),
             pltpu.SemaphoreType.DMA((lanes,)),
         ],
         compiler_params=pltpu.CompilerParams(collective_id=0, has_side_effects=True),
-    )(pair_lists, move_plan, patches, column, row)
+    )(table, above_table, before_table, patches, column, row)
     return (surfaces, peaks[:, None, :slots])
 
 

time: 98.8 us -> 95.3 us (0.965)
  Pallas kernels: 94.1 us -> 78.9 us
  starting transfers between devices: 0 us -> 8.34 us
  local copies, waits for them, and re-layouts: 3.92 us -> 5.84 us
  waiting for transfers between devices: 0 us -> 1.28 us
    pallas_call x1, Pallas kernels: 94.1 us -> 78.9 us  [body(): pl.pallas_call(functools.partial(stitch_kernel, (tiles, sections, per_pee...]
    ppermute x0 -> x2, starting transfers between devices: none -> 8.34 us  [passed_on(): lax.ppermute(value, axis, [(source, source + 1) for source in range(count...]
    unnamed x1 -> x8, local copies, waits for them, and re-layouts: 2.73 us -> 4.02 us
    ppermute x0 -> x2, waiting for transfers between devices: none -> 1.28 us  [passed_on(): lax.ppermute(value, axis, [(source, source + 1) for source in range(count...]
  transfers between devices with their start and end apart: 0 -> 2, of which waited for: 0 -> 1; matrix products, arithmetic and copies ran while one was open for 0% -> 0% of each run, Pallas kernels for 0% -> 0%
where the time goes in v3:
time: 95.3 us; the launch traced here: 95 us
  Pallas kernels  78.9 us (83%)
  starting transfers between devices  8.34 us (9%)
  local copies, waits for them, and re-layouts  5.84 us (6%)
  waiting for transfers between devices  1.28 us (1%)
    pallas_call x1, Pallas kernels, body(): pl.pallas_call(functools.partial(stitch_kernel, (tiles, sections, per_pee...  78.9 us
    ppermute x2, starting transfers between devices, passed_on(): lax.ppermute(value, axis, [(source, source + 1) for source in range(count...  8.34 us
    unnamed x8, local copies, waits for them, and re-layouts  4.02 us
  transfers between devices with their start and end apart: 2, of which 1 were waited for; matrix products, arithmetic and copies ran while one was open for 0% of the time, Pallas kernels for 0%

profile of v3, /device:TPU:0, one launch (start us, length us, event | category | flops | bytes accessed | tf_op | source)
XLA Modules:
  0.0 95.0 jit_solution(1264895287896762820)
XLA Ops:
  0.6 0.7 constant_dynamic-update-slice_fusion.1
  1.3 0.7 constant_dynamic-update-slice_fusion.table_ref
  2.0 0.0 copy-start
  2.0 4.9 %collective-permute-start.1 = (s32[5,1,1,12]{3,2,1,0:T(1,128)S(1)}, s32[5,1,1,12]{3,2,1,0:T(1,128)S(1)}, u32[]{:S(2)}, u32[]{:S(2)}) collective-permute-start(s32[5,1,1,12]{3,2,1,0:T(1,128)S(1)} %constant_dynamic-update-slice_fusion.table_ref), channel_id=1, source_target_pairs={{0,2},{1,3},{4,6},{5,7},{8,10},{9,11},{12,14},{13,15},{16,18},{17,... | collective-permute-start | bytes 728 | tf_op jit(solution)/shard_map/ppermute | solution.py:116
  6.9 3.5 %collective-permute-start = (s32[5,1,1,12]{3,2,1,0:T(1,128)S(1)}, s32[5,1,1,12]{3,2,1,0:T(1,128)S(1)}, u32[]{:S(2)}, u32[]{:S(2)}) collective-permute-start(s32[5,1,1,12]{3,2,1,0:T(1,128)S(1)} %constant_dynamic-update-slice_fusion.table_ref), channel_id=1, source_target_pairs={{0,4},{4,8},{8,12},{1,5},{5,9},{9,13},{2,6},{6,10},{10,14},{3,7},{... | collective-permute-start | bytes 728 | tf_op jit(solution)/shard_map/ppermute | solution.py:116
  10.4 0.0 collective-permute-done.1.before_table_ref
  10.4 0.0 copy-start.1
  10.4 1.3 %collective-permute-done.above_table_ref = s32[5,1,1,12]{3,2,1,0:T(1,128)S(1)} collective-permute-done((s32[5,1,1,12]{3,2,1,0:T(1,128)S(1)}, s32[5,1,1,12]{3,2,1,0:T(1,128)S(1)}, u32[]{:S(2)}, u32[]{:S(2)}) %collective-permute-start) | collective-permute-done | bytes 272 | tf_op jit(solution)/shard_map/ppermute | solution.py:116
  11.7 0.0 copy-done
  11.7 0.0 copy-done.1
  11.7 0.0 copy-start.2
  11.7 0.6 copy-done.2
  12.3 78.9 %shard_map.68 = (f32[1,1,6,256,256]{4,3,2,1,0:T(8,128)}, f32[1,128]{1,0:T(1,128)}) custom-call(s32[5,1,1,12]{3,2,1,0:T(1,128)} %copy-done, s32[5,1,1,12]{3,2,1,0:T(1,128)} %copy-done.2, s32[5,1,1,12]{3,2,1,0:T(1,128)} %copy-done.1, bf16[1,1,16,256,256]{4,3,2,1,0:T(8,128)(2,1)} %own_ref.1, bf16[2,256,256]{2,1,0:T(8,128)(2,1)} %constant.4.clone.column_ref, ...), custom_call_target="tpu_custom_call" | custom-call | tf_op jit(solution)/shard_map/pallas_call | solution.py:335
  91.2 1.1 %slice_bitcast_fusion = f32[1,1,12]{2,1,0:T(1,128)} fusion(f32[1,128]{1,0:T(1,128)} %get-tuple-element.5), kind=kLoop, calls=%fused_computation.2 | loop fusion | bytes 96 | tf_op jit(solution)/shard_map/broadcast_in_dim | solution.py:361
  92.3 2.7 %copy.9 = f32[1,1,6,256,256]{4,3,2,1,0:T(8,128)} copy(f32[1,1,6,256,256]{4,3,2,1,0:T(8,128)} %get-tuple-element.8) | data formatting | bytes 3145728
Async XLA Ops:
  2.0 9.7 %copy-start = (s32[5,1,1,12]{3,2,1,0:T(1,128)}, s32[5,1,1,12]{3,2,1,0:T(1,128)S(1)}, u32[]{:S(2)}) copy-start(s32[5,1,1,12]{3,2,1,0:T(1,128)S(1)} %constant_dynamic-update-slice_fusion.table_ref) | copy-start | bytes 724
  2.0 8.4 %collective-permute-start.1 = (s32[5,1,1,12]{3,2,1,0:T(1,128)S(1)}, s32[5,1,1,12]{3,2,1,0:T(1,128)S(1)}, u32[]{:S(2)}, u32[]{:S(2)}) collective-permute-start(s32[5,1,1,12]{3,2,1,0:T(1,128)S(1)} %constant_dynamic-update-slice_fusion.table_ref), channel_id=1, source_target_pairs={{0,2},{1,3},{4,6},{5,7},{8,10},{9,11},{12,14},{13,15},{16,18},{17,... | collective-permute-start | bytes 728 | tf_op jit(solution)/shard_map/ppermute | solution.py:116
  6.9 4.8 %collective-permute-start = (s32[5,1,1,12]{3,2,1,0:T(1,128)S(1)}, s32[5,1,1,12]{3,2,1,0:T(1,128)S(1)}, u32[]{:S(2)}, u32[]{:S(2)}) collective-permute-start(s32[5,1,1,12]{3,2,1,0:T(1,128)S(1)} %constant_dynamic-update-slice_fusion.table_ref), channel_id=1, source_target_pairs={{0,4},{4,8},{8,12},{1,5},{5,9},{9,13},{2,6},{6,10},{10,14},{3,7},{... | collective-permute-start | bytes 728 | tf_op jit(solution)/shard_map/ppermute | solution.py:116
  10.4 1.3 %copy-start.1 = (s32[5,1,1,12]{3,2,1,0:T(1,128)}, s32[5,1,1,12]{3,2,1,0:T(1,128)S(1)}, u32[]{:S(2)}) copy-start(s32[5,1,1,12]{3,2,1,0:T(1,128)S(1)} %collective-permute-done.1.before_table_ref) | copy-start | bytes 724
  11.7 0.6 copy-start.2

commit v4 on v3

--- a/solution.py
+++ b/solution.py
@@ -111,34 +111,33 @@
     return left_product(column_ref, right_product(packed * scale, row_ref))
 
 
-def passed_on(value, axis):
-    count = lax.axis_size(axis)
-    return lax.ppermute(value, axis, [(source, source + 1) for source in range(count - 1)])
-
-
-def slot_of(table_ref, target, position):
+def slot_of(plan_ref, target, position):
     def look(slot, carried):
         seen, chosen, used = carried
-        hit = (table_ref[3, 0, 0, slot] == target).astype(jnp.int32)
+        hit = (plan_ref[0, 0, 0, slot] == target).astype(jnp.int32)
         match = hit * (seen == position).astype(jnp.int32)
         return (seen + hit, chosen + match * slot, used + match)
 
     zero = jnp.int32(0)
-    slots = table_ref.shape[-1]
+    slots = plan_ref.shape[-1]
     _, chosen, used = lax.fori_loop(0, slots, look, (zero, zero, zero), unroll=True)
     return chosen, used
 
 
 def stitch_kernel(
     sizes,
-    table_ref,
-    above_table_ref,
-    before_table_ref,
-    own_ref,
+    lists_ref,
+    plan_ref,
+    patches_ref,
     column_ref,
     row_ref,
     surface_ref,
     peak_ref,
+    own_ref,
+    above_lists_ref,
+    above_plan_ref,
+    before_lists_ref,
+    before_plan_ref,
     to_above_ref,
     to_before_ref,
     below_ref,
@@ -147,6 +146,9 @@
     sent_note_ref,
     got_ref,
     got_note_ref,
+    load_sem,
+    list_send,
+    list_recv,
     fetch_send,
     fetch_recv,
     code_send,
@@ -158,6 +160,8 @@
     tile, sect = lax.axis_index("tile"), lax.axis_index("sect")
     lanes = tiles * per_peer
 
+    load = pltpu.make_async_copy(patches_ref.at[0, 0], own_ref, load_sem)
+    load.start()
     barrier = pltpu.get_barrier_semaphore()
     for shift in range(1, tiles):
         pl.semaphore_signal(
@@ -175,18 +179,42 @@
     neighbours = lax.min(sect, 1) + lax.min(sections - 1 - sect, 1)
     pl.semaphore_wait(barrier, tiles - 1 + neighbours)
 
+    def list_copies(axis, place, refs, first_sem):
+        return [
+            pltpu.make_async_remote_copy(
+                src_ref=source,
+                dst_ref=target,
+                send_sem=list_send.at[first_sem + index],
+                recv_sem=list_recv.at[first_sem + index],
+                device_id={axis: place},
+                device_id_type=MESH,
+            )
+            for index, (source, target) in enumerate(zip((lists_ref, plan_ref), refs))
+        ]
+
+    to_below = list_copies(
+        "tile", lax.min(tile + 1, tiles - 1), (above_lists_ref, above_plan_ref), 0
+    )
+    to_next = list_copies(
+        "sect", lax.min(sect + 1, sections - 1), (before_lists_ref, before_plan_ref), 2
+    )
+
+    @pl.when(tile < tiles - 1)
+    def _():
+        for copy in to_below:
+            copy.start()
+
+    @pl.when(sect < sections - 1)
+    def _():
+        for copy in to_next:
+            copy.start()
+
+    surface_ref[...] = jnp.zeros_like(surface_ref)
+    peak_ref[...] = jnp.zeros_like(peak_ref)
+    load.wait()
+
     def target_of(owner_tile, lane):
         return lax.rem(owner_tile + tiles - 1 - lane // per_peer, tiles)
-
-    def stage(lane, carried):
-        position = lax.rem(lane, per_peer)
-        slot, _ = slot_of(above_table_ref, target_of(tile + tiles - 1, lane), position)
-        to_above_ref[lane] = own_ref[0, 0, above_table_ref[2, 0, 0, slot]]
-        slot, _ = slot_of(before_table_ref, target_of(tile, lane), position)
-        to_before_ref[lane] = own_ref[0, 0, before_table_ref[2, 0, 0, slot]]
-        return carried
-
-    lax.fori_loop(0, lanes, stage, 0)
 
     def to_above(lane):
         return pltpu.make_async_remote_copy(
@@ -208,20 +236,43 @@
             device_id_type=MESH,
         )
 
-    def send_patches(lane, carried):
-        @pl.when(tile > 0)
-        def _():
+    @pl.when(tile > 0)
+    def _():
+        for copy in to_below:
+            copy.wait_recv()
+
+        def stage(lane, carried):
+            slot, _ = slot_of(
+                above_plan_ref, target_of(tile + tiles - 1, lane), lax.rem(lane, per_peer)
+            )
+            to_above_ref[lane] = own_ref[above_lists_ref[2, 0, 0, slot]]
+            return carried
+
+        lax.fori_loop(0, lanes, stage, 0)
+
+        def send(lane, carried):
             to_above(lane).start()
-
-        @pl.when(sect > 0)
-        def _():
+            return carried
+
+        lax.fori_loop(0, lanes, send, 0)
+
+    @pl.when(sect > 0)
+    def _():
+        for copy in to_next:
+            copy.wait_recv()
+
+        def stage(lane, carried):
+            slot, _ = slot_of(before_plan_ref, target_of(tile, lane), lax.rem(lane, per_peer))
+            to_before_ref[lane] = own_ref[before_lists_ref[2, 0, 0, slot]]
+            return carried
+
+        lax.fori_loop(0, lanes, stage, 0)
+
+        def send(lane, carried):
             to_before(lane).start()
-
-        return carried
-
-    lax.fori_loop(0, lanes, send_patches, 0)
-    surface_ref[...] = jnp.zeros_like(surface_ref)
-    peak_ref[...] = jnp.zeros_like(peak_ref)
+            return carried
+
+        lax.fori_loop(0, lanes, send, 0)
 
     def copies(lane, target):
         code = pltpu.make_async_remote_copy(
@@ -242,7 +293,7 @@
         )
         return code, note
 
-    slot_ids = lax.broadcasted_iota(jnp.int32, peak_ref.shape, 1)
+    slot_ids = lax.broadcasted_iota(jnp.int32, peak_ref.shape, 2)
 
     def settle(code, note):
         found = code.astype(jnp.int32).astype(jnp.float32) * note[0:1]
@@ -255,9 +306,9 @@
     def correlate_lane(lane, carried):
         shift = tiles - 1 - lane // per_peer
         target = target_of(tile, lane)
-        slot, used = slot_of(table_ref, target, lax.rem(lane, per_peer))
-        kind = table_ref[0, 0, 0, slot]
-        first = own_ref[0, 0, table_ref[1, 0, 0, slot]]
+        slot, used = slot_of(plan_ref, target, lax.rem(lane, per_peer))
+        kind = lists_ref[0, 0, 0, slot]
+        first = own_ref[lists_ref[1, 0, 0, slot]]
 
         @pl.when(tile < tiles - 1)
         def _():
@@ -273,7 +324,7 @@
         peak_ref[...] = jnp.where(
             (slot_ids == slot) & (used > 0), jnp.full(peak_ref.shape, peak), peak_ref[...]
         )
-        place = jnp.where(used > 0, table_ref[4, 0, 0, slot], -1).astype(jnp.float32)
+        place = jnp.where(used > 0, plan_ref[1, 0, 0, slot], -1).astype(jnp.float32)
         tallest = jnp.max(jnp.abs(surface), axis=0, keepdims=True)
         tallest = jnp.maximum(tallest, SMALLEST)
         code = jnp.round(surface * (STEPS / tallest)).astype(jnp.int32).astype(jnp.int16)
@@ -318,6 +369,16 @@
         return carried
 
     lax.fori_loop(0, lanes, patches_left, 0)
+
+    @pl.when(tile < tiles - 1)
+    def _():
+        for copy in to_below:
+            copy.wait_send()
+
+    @pl.when(sect < sections - 1)
+    def _():
+        for copy in to_next:
+            copy.wait_send()
 
 
 def body(patches, pair_lists, move_plan):
@@ -328,19 +389,22 @@
     per_peer = (slots + tiles - 1) // tiles
     lanes = tiles * per_peer
     column, row = real_tables(length)
-    table = jnp.concatenate([pair_lists, move_plan], axis=0)
-    above_table, before_table = passed_on(table, "tile"), passed_on(table, "sect")
     vmem = pl.BlockSpec(memory_space=pltpu.VMEM)
     smem = pl.BlockSpec(memory_space=pltpu.SMEM)
     surfaces, peaks = pl.pallas_call(
         functools.partial(stitch_kernel, (tiles, sections, per_peer, works)),
-        in_specs=[smem, smem, smem, vmem, vmem, vmem],
+        in_specs=[smem, smem, pl.BlockSpec(memory_space=pl.ANY), vmem, vmem],
         out_specs=[vmem, vmem],
         out_shape=[
             jax.ShapeDtypeStruct((1, 1, works, length, length), jnp.float32),
-            jax.ShapeDtypeStruct((1, 128), jnp.float32),
+            jax.ShapeDtypeStruct((1, 1, slots), jnp.float32),
         ],
         scratch_shapes=[
+            pltpu.VMEM(patches.shape[2:], jnp.bfloat16),
+            pltpu.SMEM(pair_lists.shape, jnp.int32),
+            pltpu.SMEM(move_plan.shape, jnp.int32),
+            pltpu.SMEM(pair_lists.shape, jnp.int32),
+            pltpu.SMEM(move_plan.shape, jnp.int32),
             pltpu.VMEM((lanes, length, length), jnp.bfloat16),
             pltpu.VMEM((lanes, length, length), jnp.bfloat16),
             pltpu.VMEM((lanes, length, length), jnp.bfloat16),
@@ -349,6 +413,9 @@
             pltpu.VMEM((lanes, 8, length), jnp.float32),
             pltpu.VMEM((lanes, length, length), jnp.int16),
             pltpu.VMEM((lanes, 8, length), jnp.float32),
+            pltpu.SemaphoreType.DMA(()),
+            pltpu.SemaphoreType.DMA((4,)),
+            pltpu.SemaphoreType.DMA((4,)),
             pltpu.SemaphoreType.DMA((2, lanes)),
             pltpu.SemaphoreType.DMA((2, lanes)),
             pltpu.SemaphoreType.DMA((lanes,)),
@@ -357,8 +424,8 @@
             pltpu.SemaphoreType.DMA((lanes,)),
         ],
         compiler_params=pltpu.CompilerParams(collective_id=0, has_side_effects=True),
-    )(table, above_table, before_table, patches, column, row)
-    return (surfaces, peaks[:, None, :slots])
+    )(pair_lists, move_plan, patches, column, row)
+    return (surfaces, peaks)
 
 
 def solution(mesh):

time: 95.3 us -> 86.1 us (0.903)
  starting transfers between devices: 8.34 us -> 0 us
  Pallas kernels: 78.9 us -> 82 us
  local copies, waits for them, and re-layouts: 5.84 us -> 3.25 us
  waiting for transfers between devices: 1.28 us -> 0 us
    ppermute x2 -> x0, starting transfers between devices: 8.34 us -> none  [passed_on(): lax.ppermute(value, axis, [(source, source + 1) for source in range(count...]
    pallas_call x1, Pallas kernels: 78.9 us -> 82 us  [body(): pl.pallas_call(functools.partial(stitch_kernel, (tiles, sections, per_pee...]
    ppermute x2 -> x0, waiting for transfers between devices: 1.28 us -> none  [passed_on(): lax.ppermute(value, axis, [(source, source + 1) for source in range(count...]
    broadcast_in_dim x1 -> x0, local copies, waits for them, and re-layouts: 1.14 us -> none  [body(): return (surfaces, peaks[:, None, :slots])]
    unnamed x8 -> x4, local copies, waits for them, and re-layouts: 4.02 us -> 3.25 us
  transfers between devices with their start and end apart: 2 -> 0, of which waited for: 1 -> 0; matrix products, arithmetic and copies ran while one was open for 0% -> 0% of each run, Pallas kernels for 0% -> 0%
where the time goes in v4:
time: 86.1 us; the launch traced here: 85.9 us
  Pallas kernels  82 us (95%)
  local copies, waits for them, and re-layouts  3.25 us (4%)
    pallas_call x1, Pallas kernels, body(): pl.pallas_call(functools.partial(stitch_kernel, (tiles, sections, per_pee...  82 us
    unnamed x4, local copies, waits for them, and re-layouts  3.25 us

profile of v4, /device:TPU:0, one launch (start us, length us, event | category | flops | bytes accessed | tf_op | source)
XLA Modules:
  0.0 85.9 jit_solution(3986144414731454278)
XLA Ops:
  0.6 82.0 %shard_map.68 = (f32[1,1,6,256,256]{4,3,2,1,0:T(8,128)}, f32[1,1,12]{2,1,0:T(1,128)}) custom-call(s32[3,1,1,12]{3,2,1,0:T(1,128)} %lists_ref.1, s32[2,1,1,12]{3,2,1,0:T(1,128)} %plan_ref.1, bf16[1,1,16,256,256]{4,3,2,1,0:T(8,128)(2,1)} %patches_ref.1, bf16[2,256,256]{2,1,0:T(8,128)(2,1)} %constant.4.clone.column_ref, bf16[2,256,256]{2,1,0:T(8,128)(2,1)} %constant.5.clone.row_ref), custom_call_target="tpu_custom_call" | custom-call | tf_op jit(solution)/shard_map/pallas_call | solution.py:394
  82.6 0.0 copy-start
  82.6 2.7 %copy.9 = f32[1,1,6,256,256]{4,3,2,1,0:T(8,128)} copy(f32[1,1,6,256,256]{4,3,2,1,0:T(8,128)} %get-tuple-element.4) | data formatting | bytes 3145728
  85.4 0.0 copy-done
  85.4 0.5 copy.10
Async XLA Ops:
  82.6 2.7 %copy-start = (f32[1,1,12]{2,1,0:T(1,128)S(1)}, f32[1,1,12]{2,1,0:T(1,128)}, u32[]{:S(2)}) copy-start(f32[1,1,12]{2,1,0:T(1,128)} %get-tuple-element.5) | copy-start | bytes 148

commit v5 on v4

--- a/solution.py
+++ b/solution.py
@@ -214,7 +214,9 @@
     load.wait()
 
     def target_of(owner_tile, lane):
-        return lax.rem(owner_tile + tiles - 1 - lane // per_peer, tiles)
+        block = lane // per_peer
+        passed = lax.max(lax.min(block - owner_tile + 1, 1), 0)
+        return block + passed - (tiles - owner_tile) * (block // (tiles - 1))
 
     def to_above(lane):
         return pltpu.make_async_remote_copy(
@@ -243,7 +245,7 @@
 
         def stage(lane, carried):
             slot, _ = slot_of(
-                above_plan_ref, target_of(tile + tiles - 1, lane), lax.rem(lane, per_peer)
+                above_plan_ref, target_of(tile - 1, lane), lax.rem(lane, per_peer)
             )
             to_above_ref[lane] = own_ref[above_lists_ref[2, 0, 0, slot]]
             return carried
@@ -274,20 +276,20 @@
 
         lax.fori_loop(0, lanes, send, 0)
 
-    def copies(lane, target):
+    def copies(lane, target, place):
         code = pltpu.make_async_remote_copy(
             src_ref=sent_ref.at[lane],
-            dst_ref=got_ref.at[lane],
+            dst_ref=got_ref.at[place],
             send_sem=code_send.at[lane],
-            recv_sem=code_recv.at[lane],
+            recv_sem=code_recv.at[place],
             device_id={"tile": target},
             device_id_type=MESH,
         )
         note = pltpu.make_async_remote_copy(
             src_ref=sent_note_ref.at[lane],
-            dst_ref=got_note_ref.at[lane],
+            dst_ref=got_note_ref.at[place],
             send_sem=note_send.at[lane],
-            recv_sem=note_recv.at[lane],
+            recv_sem=note_recv.at[place],
             device_id={"tile": target},
             device_id_type=MESH,
         )
@@ -304,7 +306,6 @@
             )
 
     def correlate_lane(lane, carried):
-        shift = tiles - 1 - lane // per_peer
         target = target_of(tile, lane)
         slot, used = slot_of(plan_ref, target, lax.rem(lane, per_peer))
         kind = lists_ref[0, 0, 0, slot]
@@ -332,9 +333,11 @@
         note_row = lax.broadcasted_iota(jnp.int32, sent_note_ref.shape[1:], 0)
         sent_note_ref[lane] = jnp.where(note_row == 0, tallest * (1.0 / STEPS), place)
 
-        @pl.when(shift > 0)
+        @pl.when(lane < lanes - per_peer)
         def _():
-            code_copy, note_copy = copies(lane, target)
+            code_copy, note_copy = copies(
+                lane, target, tile * per_peer + lax.rem(lane, per_peer)
+            )
             note_copy.start()
             code_copy.start()
 
@@ -349,10 +352,12 @@
     lax.fori_loop(lanes - per_peer, lanes, settle_own, 0)
 
     def settle_lane(lane, carried):
-        code_copy, note_copy = copies(lane, target_of(tile, lane))
+        source = target_of(tile, lane)
+        place = source * per_peer + lax.rem(lane, per_peer)
+        code_copy, note_copy = copies(lane, source, place)
         note_copy.wait()
         code_copy.wait()
-        settle(got_ref[lane], got_note_ref[lane])
+        settle(got_ref[place], got_note_ref[place])
         return carried
 
     lax.fori_loop(0, lanes - per_peer, settle_lane, 0)
@@ -410,9 +415,9 @@
             pltpu.VMEM((lanes, length, length), jnp.bfloat16),
             pltpu.VMEM((lanes, length, length), jnp.bfloat16),
             pltpu.VMEM((lanes, length, length), jnp.int16),
-            pltpu.VMEM((lanes, 8, length), jnp.float32),
+            pltpu.VMEM((lanes, 2, length), jnp.float32),
             pltpu.VMEM((lanes, length, length), jnp.int16),
-            pltpu.VMEM((lanes, 8, length), jnp.float32),
+            pltpu.VMEM((lanes, 2, length), jnp.float32),
             pltpu.SemaphoreType.DMA(()),
             pltpu.SemaphoreType.DMA((4,)),
             pltpu.SemaphoreType.DMA((4,)),

time: 86.1 us -> 82.2 us (0.955)
  the two profiles are of different devices: /device:TPU:0 before, /device:TPU:8 now
where the time goes in v5:
time: 82.2 us; the launch traced here: 82 us
  Pallas kernels  78.1 us (95%)
  local copies, waits for them, and re-layouts  3.25 us (4%)
    pallas_call x1, Pallas kernels, body(): pl.pallas_call(functools.partial(stitch_kernel, (tiles, sections, per_pee...  78.1 us
    unnamed x4, local copies, waits for them, and re-layouts  3.25 us

profile of v5, /device:TPU:8, one launch (start us, length us, event | category | flops | bytes accessed | tf_op | source)
XLA Modules:
  0.0 82.0 jit_solution(6323119778999343794)
XLA Ops:
  0.6 78.1 %shard_map.68 = (f32[1,1,6,256,256]{4,3,2,1,0:T(8,128)}, f32[1,1,12]{2,1,0:T(1,128)}) custom-call(s32[3,1,1,12]{3,2,1,0:T(1,128)} %lists_ref.1, s32[2,1,1,12]{3,2,1,0:T(1,128)} %plan_ref.1, bf16[1,1,16,256,256]{4,3,2,1,0:T(8,128)(2,1)} %patches_ref.1, bf16[2,256,256]{2,1,0:T(8,128)(2,1)} %constant.4.clone.column_ref, bf16[2,256,256]{2,1,0:T(8,128)(2,1)} %constant.5.clone.row_ref), custom_call_target="tpu_custom_call" | custom-call | tf_op jit(solution)/shard_map/pallas_call | solution.py:399
  78.8 0.0 copy-start
  78.8 2.7 %copy.9 = f32[1,1,6,256,256]{4,3,2,1,0:T(8,128)} copy(f32[1,1,6,256,256]{4,3,2,1,0:T(8,128)} %get-tuple-element.4) | data formatting | bytes 3145728
  81.5 0.0 copy-done
  81.5 0.5 copy.10
Async XLA Ops:
  78.8 2.7 %copy-start = (f32[1,1,12]{2,1,0:T(1,128)S(1)}, f32[1,1,12]{2,1,0:T(1,128)}, u32[]{:S(2)}) copy-start(f32[1,1,12]{2,1,0:T(1,128)} %get-tuple-element.5) | copy-start | bytes 148
